TPU v7x, 256 devices: a whole 4x4x8 slice. The times are simulated.
256 devices in a mesh: dp: 32 (over x, z), seq: 8 (over y, core).
Axes of the slice: x: 4, y: 4, z: 8, core: 2. Of those that a mesh axis runs over, the one named last changes fastest.
Arguments:
- words: bfloat16 [128, 1024, 1024], P('dp', 'seq'), may hold values from -6 to 6
- patches: bfloat16 [128, 2048, 1024], P('dp', 'seq'), may hold values from -6 to 6
- proj: bfloat16 [1024, 1024], P('dp'), may hold values from -0.1875 to 0.1875
- routes: int32 [128, 1024, 1], P('dp', 'seq'), may hold values from 0 to 7; in each aligned block of 128 rows (0 to 127, 128 to 255, ..., all dimensions but the last counted through in order) at most 32 rows name the same one
- targets: int32 [128, 1024], P('dp', 'seq'), may hold values from 0 to 255
- counts: int32 [128], P('dp'), may hold values from 512 to 1024
- flags: int32 [128, 16, 32], P('dp'), may hold values 0 or 1
Outputs:
- word_loss: float32 [128, 1024], P('dp', 'seq')
- proj_grad: float32 [1024, 1024], P('dp', 'seq')
Inputs may be any that keep to these rules, and one draw needn't show every extreme that they name: `routes`: among the 128 words of one page held by one index of seq, at most 32 name the same shard; some block reaches 32.
All inputs are finite; a program needn't handle non-finite values. No bound on the sum of `flags` on one device may be relied on, other than what follows from the above.
Results may differ from a plain program's by a relative error of at most 0.0065.
Values may be sent and summed in bfloat16 or wider, within the bound.
A program may use at most 64 MiB of HBM per device.

v0:
```python
import math

import jax
import jax.numpy as jnp
from jax import lax
from jax.sharding import PartitionSpec as P

MARGIN_BLOCK_SIZE = 64


def local(words, patches, proj, routes, targets, counts, flags):
    pages, wdev, width = words.shape
    ppsz = patches.shape[1]
    nblk = flags.shape[1]
    nseq = lax.axis_size("seq")
    mine = lax.axis_index("seq")
    capacity_limit = 2 * wdev // nseq
    bps = ppsz // MARGIN_BLOCK_SIZE
    scale = 2.0 / math.sqrt(width)
    flat_rows = words.reshape(pages * wdev, width)
    columns = flat_rows
    query = jnp.dot(
        columns, lax.all_gather(proj, "dp", axis=0, tiled=True), preferred_element_type=jnp.float32
    )
    query = query.astype(jnp.bfloat16).reshape(pages, wdev, width)
    destination_slot = routes[:, :, 0]
    onehot = (
        destination_slot[:, :, None] == jnp.arange(nseq, dtype=jnp.int32)[None, None, :]
    ).astype(jnp.int32)
    rank = jnp.cumsum(onehot, axis=1) - onehot
    slot = jnp.sum(rank * onehot, axis=2)
    slot_hit = (
        slot[:, :, None] == jnp.arange(capacity_limit, dtype=jnp.int32)[None, None, :]
    ).astype(jnp.int32)
    dispatch = onehot[:, :, :, None] * slot_hit[:, :, None, :]
    dispatch_bf = dispatch.astype(jnp.bfloat16)
    word_idx = mine * wdev + jnp.arange(wdev, dtype=jnp.int32)
    q_buf = jnp.einsum(
        "pwhc,pwd->hpcd", dispatch_bf, query, preferred_element_type=jnp.float32
    ).astype(jnp.bfloat16)
    tgt_buf = jnp.einsum("pwhc,pw->hpc", dispatch, targets)
    idx_buf = jnp.einsum("pwhc,w->hpc", dispatch, word_idx + 1) - 1
    q_in, tgt_in, idx_in = (
        lax.all_to_all(q_buf, "seq", split_axis=0, concat_axis=0, tiled=True),
        lax.all_to_all(tgt_buf, "seq", split_axis=0, concat_axis=0, tiled=True),
        lax.all_to_all(idx_buf, "seq", split_axis=0, concat_axis=0, tiled=True),
    )
    scores = jnp.einsum("hpcd,pkd->hpck", q_in, patches, preferred_element_type=jnp.float32) * scale
    own = lax.dynamic_slice_in_dim(flags, mine * bps, bps, 2)
    word_block = jnp.maximum(idx_in, 0) // MARGIN_BLOCK_SIZE
    picked = (word_block[..., None] == jnp.arange(nblk, dtype=jnp.int32)).astype(jnp.int32)
    hit = jnp.sum(picked[..., None] * own[None, :, None, :, :], axis=-2)
    allowed = (hit > 0) | (
        (tgt_in // MARGIN_BLOCK_SIZE)[..., None] == jnp.arange(bps, dtype=jnp.int32)
    )
    mask = jnp.broadcast_to(allowed[..., None], allowed.shape + (MARGIN_BLOCK_SIZE,)).reshape(
        scores.shape
    )
    expo = jnp.where(mask, jnp.exp(scores), jnp.float32(0.0))
    total = jnp.sum(expo, axis=-1)
    is_target = jnp.arange(ppsz, dtype=jnp.int32) == tgt_in[..., None]
    target_score = jnp.sum(jnp.where(is_target, scores, jnp.float32(0.0)), axis=-1)
    valid_mask = (idx_in >= 0) & (idx_in < counts[None, :, None])
    loss_out = jnp.where(valid_mask, jnp.log(total) - target_score, jnp.float32(0.0))
    coef = jnp.where(
        valid_mask, jnp.float32(64.0) / counts.astype(jnp.float32)[None, :, None], jnp.float32(0.0)
    )
    dscore = (coef[..., None] * (expo / total[..., None] - is_target.astype(jnp.float32))).astype(
        jnp.bfloat16
    )
    dquery = (
        jnp.einsum("hpck,pkd->hpcd", dscore, patches, preferred_element_type=jnp.float32) * scale
    ).astype(jnp.bfloat16)
    loss_home = lax.all_to_all(loss_out, "seq", split_axis=0, concat_axis=0, tiled=True)
    dq_home = lax.all_to_all(dquery, "seq", split_axis=0, concat_axis=0, tiled=True)
    right = (
        jnp.einsum("pwhc,hpcd->pwd", dispatch_bf, dq_home, preferred_element_type=jnp.float32)
        .astype(jnp.bfloat16)
        .reshape(-1, width)
    )
    word_loss = jnp.einsum("pwhc,hpc->pw", dispatch.astype(jnp.float32), loss_home)
    columns = flat_rows
    partial_rows = lax.psum_scatter(
        jnp.einsum("rc,rd->cd", columns, right, preferred_element_type=jnp.float32),
        "dp",
        scatter_dimension=0,
        tiled=True,
    )
    proj_grad = lax.psum_scatter(partial_rows, "seq", scatter_dimension=1, tiled=True)
    return (word_loss, proj_grad)


def solution(mesh):
    in_specs = (
        P("dp", "seq", None),
        P("dp", "seq", None),
        P("dp", None),
        P("dp", "seq", None),
        P("dp", "seq"),
        P("dp"),
        P("dp", None, None),
    )
    out_specs = (P("dp", "seq"), P("dp", "seq"))
    return jax.shard_map(local, mesh=mesh, in_specs=in_specs, out_specs=out_specs, check_vma=False)
```

profile of v0, /device:TPU:24, one launch (start us, length us, event | category | flops | bytes accessed | tf_op | source)
XLA Modules:
  0.0 437.7 jit_solution(18329256724800153465)
XLA Ops:
  7.2 0.0 copy-start
  7.2 0.0 all-gather.2.cloned.1.call-start
  7.2 0.7 all-gather.2.cloned.1.call-update
  7.9 0.8 fusion.37
  8.7 0.1 copy.34
  8.8 0.3 reduce_window_sum.11
  9.1 0.9 select_reduce_fusion.1
  10.0 3.5 fusion.25
  13.6 0.7 reshape.58
  14.2 5.2 %all-to-all-start = ((s32[8,1,128]{2,1,0:T(1,128)}), s32[8,1,128]{2,1,0:T(1,128)S(1)}, u32[]{:S(2)}, u32[]{:S(2)}) async-start(s32[8,1,128]{2,1,0:T(1,128)} %reshape.58), calls=%async_computation | async-start | bytes 8192 | tf_op jit(solution)/shard_map/all_to_all | solution.py:46
  19.5 4.2 fusion.23
  23.6 0.7 reshape.60
  24.3 66.9 %all-gather.2.cloned.1.call-done = bf16[1024,1024]{1,0:T(8,128)(2,1)} async-done(((bf16[32,1024]{1,0:T(8,128)(2,1)}), bf16[1024,1024]{1,0:T(8,128)(2,1)}) %all-gather.2.cloned.1.call-update) | async-done | bytes 2097168 | tf_op jit(solution)/shard_map/all_gather | solution.py:23
  91.2 4.2 convolution_convert_fusion
  95.4 0.0 all-to-all-done
  95.4 4.8 %all-to-all-start.1 = ((s32[8,1,128]{2,1,0:T(1,128)}), s32[8,1,128]{2,1,0:T(1,128)S(1)}, u32[]{:S(2)}, u32[]{:S(2)}) async-start(s32[8,1,128]{2,1,0:T(1,128)} %reshape.60), calls=%async_computation.1 | async-start | bytes 8192 | tf_op jit(solution)/shard_map/all_to_all | solution.py:45
  100.2 3.3 convert_bitcast_fusion
  103.4 0.0 all-to-all-done.1
  103.4 6.3 %all-to-all-start.2 = ((bf16[8,4,32,1024]{3,2,1,0:T(8,128)(2,1)}), bf16[8,4,32,1024]{3,2,1,0:T(8,128)(2,1)}, u32[]{:S(2)}, u32[]{:S(2)}) async-start(bf16[8,4,32,1024]{3,2,1,0:T(8,128)(2,1)} %convert_bitcast_fusion), calls=%async_computation.2 | async-start | bytes 4194304 | tf_op jit(solution)/shard_map/all_to_all | solution.py:44
  109.7 0.1 constant_dynamic-slice_fusion
  109.8 0.1 copy.39
  109.9 0.5 broadcast.80
  110.4 0.7 reduce
  111.1 0.1 reshape.59
  111.2 0.7 reduce.1
  111.9 0.1 reshape.61
  112.0 0.3 multiply_reduce_fusion
  112.4 0.3 copy.45
  112.7 1.4 broadcast_in_dim.15
  114.1 0.8 reshape.43
  114.9 0.1 broadcast_select_fusion
  114.9 20.0 %all-to-all-done.2 = bf16[8,4,32,1024]{3,2,1,0:T(8,128)(2,1)} async-done(((bf16[8,4,32,1024]{3,2,1,0:T(8,128)(2,1)}), bf16[8,4,32,1024]{3,2,1,0:T(8,128)(2,1)}, u32[]{:S(2)}, u32[]{:S(2)}) %all-to-all-start.2) | async-done | bytes 2097184 | tf_op jit(solution)/shard_map/all_to_all | solution.py:44
  134.9 0.0 copy-done
  134.9 2.7 fusion.27
  137.6 1.2 fusion.6
  138.8 0.0 copy-start.1
  138.8 30.8 %all_to_all.25 = bf16[8,4,32,1024]{3,2,1,0:T(8,128)(2,1)} all-to-all(bf16[8,4,32,1024]{3,2,1,0:T(8,128)(2,1)S(1)} %fusion.6), channel_id=1, replica_groups=mesh['dp'=32,'seq'=8] {'seq'}, dimensions={0} | all-to-all | bytes 4194304 | tf_op jit(solution)/shard_map/all_to_all | solution.py:75
  169.6 5.1 %convolution_bitcast_fusion = f32[1024,1024]{0,1:T(8,128)} fusion(bf16[4,128,1024]{2,1,0:T(8,128)(2,1)S(1)} %copy-done.1, bf16[8,4,32,1024]{3,2,1,0:T(8,128)(2,1)} %all_to_all.25, s32[4,128,32]{1,2,0:T(8,128)S(1)} %fusion.39, s32[4,128,8]{1,2,0:T(8,128)S(1)} %copy.34), kind=kOutput, calls=%fused_computation.1 | convolution fusion | flops 1342963712 | bytes 7421952 | tf_op jit(solution)/shard_map/rc,rd->cd/dot_general | solution.py:84
  174.7 5.3 %copy.63 = f32[1024,1024]{1,0:T(8,128)} copy(f32[1024,1024]{0,1:T(8,128)} %convolution_bitcast_fusion) | data formatting | bytes 8388608
  180.0 0.0 reduce-scatter.7.cloned.1.call-update
  180.1 0.0 reduce-scatter.5.cloned.1.call-start
  180.1 218.2 %reduce-scatter.7.cloned.1.call-done = f32[32,1024]{1,0:T(8,128)} async-done(((f32[1024,1024]{1,0:T(8,128)}), f32[32,1024]{1,0:T(8,128)}) %reduce-scatter.7.cloned.1.call-update) | async-done | bytes 131088
  398.3 1.9 copy.64
  400.2 0.0 reduce-scatter.5.cloned.1.call-update
  400.3 7.8 %all_to_all.26 = bf16[8,4,32]{2,1,0:T(4,128)(2,1)S(1)} all-to-all(bf16[8,4,32]{2,1,0:T(4,128)(2,1)S(1)} %copy.49), channel_id=1, replica_groups=mesh['dp'=32,'seq'=8] {'seq'}, dimensions={0} | all-to-all | bytes 4096 | tf_op jit(solution)/shard_map/all_to_all | solution.py:74
  408.1 0.8 fusion.28
  408.9 20.8 %reduce-scatter.5.cloned.1.call-done = f32[32,128]{0,1:T(8,128)} async-done(((f32[32,1024]{0,1:T(8,128)}), f32[32,128]{0,1:T(8,128)}) %reduce-scatter.5.cloned.1.call-update) | async-done | bytes 16400 | tf_op jit(solution)/shard_map/reduce_scatter | solution.py:89
  429.7 1.5 copy.53
  (18 shorter events, 0.2 us)
Async XLA Ops:
  7.2 127.8 %copy-start = (bf16[4,256,1024]{2,1,0:T(8,128)(2,1)S(1)}, bf16[4,256,1024]{2,1,0:T(8,128)(2,1)}, u32[]{:S(2)}) copy-start(bf16[4,256,1024]{2,1,0:T(8,128)(2,1)} %param.8) | copy-start | bytes 6291460
  7.2 84.0 %all-gather.2.cloned.1.call-start = ((), (), s32[]{:S(2)}) async-start(), calls=%async_computation.7 | async-start | bytes 2162688 | tf_op jit(solution)/shard_map/all_gather | solution.py:23
  14.2 81.1 %all-to-all-start = ((s32[8,1,128]{2,1,0:T(1,128)}), s32[8,1,128]{2,1,0:T(1,128)S(1)}, u32[]{:S(2)}, u32[]{:S(2)}) async-start(s32[8,1,128]{2,1,0:T(1,128)} %reshape.58), calls=%async_computation | async-start | bytes 8192 | tf_op jit(solution)/shard_map/all_to_all | solution.py:46
  95.4 8.1 %all-to-all-start.1 = ((s32[8,1,128]{2,1,0:T(1,128)}), s32[8,1,128]{2,1,0:T(1,128)S(1)}, u32[]{:S(2)}, u32[]{:S(2)}) async-start(s32[8,1,128]{2,1,0:T(1,128)} %reshape.60), calls=%async_computation.1 | async-start | bytes 8192 | tf_op jit(solution)/shard_map/all_to_all | solution.py:45
  103.4 6.3 %copy-start.2 = (s32[4,16,32]{2,1,0:T(8,128)S(1)}, s32[4,16,32]{2,1,0:T(8,128)}, u32[]{:S(2)}) copy-start(s32[4,16,32]{2,1,0:T(8,128)} %param.13) | copy-start | bytes 24580
  103.4 6.4 %copy-start.3 = (s32[4]{0:T(128)S(1)}, s32[4]{0:T(128)}, u32[]{:S(2)}) copy-start(s32[4]{0:T(128)} %param.12) | copy-start | bytes 52
  103.4 31.5 %all-to-all-start.2 = ((bf16[8,4,32,1024]{3,2,1,0:T(8,128)(2,1)}), bf16[8,4,32,1024]{3,2,1,0:T(8,128)(2,1)}, u32[]{:S(2)}, u32[]{:S(2)}) async-start(bf16[8,4,32,1024]{3,2,1,0:T(8,128)(2,1)} %convert_bitcast_fusion), calls=%async_computation.2 | async-start | bytes 4194304 | tf_op jit(solution)/shard_map/all_to_all | solution.py:44
  109.7 288.6 %reduce-scatter.7.cloned.1.call-start = ((), (), s32[]{:S(2)}) async-start(), calls=%async_computation.9 | async-start | bytes 4325376
  138.8 30.8 %copy-start.1 = (bf16[4,128,1024]{2,1,0:T(8,128)(2,1)S(1)}, bf16[4,128,1024]{2,1,0:T(8,128)(2,1)}, u32[]{:S(2)}) copy-start(bf16[4,128,1024]{2,1,0:T(8,128)(2,1)} %param.7) | copy-start | bytes 3145732
  180.1 249.6 %reduce-scatter.5.cloned.1.call-start = ((), (), s32[]{:S(2)}) async-start(), calls=%async_computation.8 | async-start | bytes 589824 | tf_op jit(solution)/shard_map/reduce_scatter | solution.py:89
Sparse Core Ops, SparseCore 0:
  10.6 80.5 all-gather.1
  180.2 218.0 reduce-scatter.6
  401.0 28.6 reduce-scatter.4
where the time goes:
time: 442 us; the launch traced here: 438 us
  waiting for transfers between devices  327 us (74%)
  blocking collectives  38.6 us (9%)
  matrix products  24.8 us (6%)
  starting transfers between devices  16.3 us (4%)
  between operations  13.9 us (3%)
  local copies, waits for them, and re-layouts  13.6 us (3%)
    unnamed x4, waiting for transfers between devices  219 us
    all_gather x1, waiting for transfers between devices, local(): lax.all_gather(proj, 'dp', axis=0, tiled=True)  66.9 us
    all_to_all x1, blocking collectives, local(): lax.all_to_all(dquery, 'seq', split_axis=0, concat_axis=0, tiled=True)  30.8 us
    reduce_scatter x1, waiting for transfers between devices, local(): lax.psum_scatter(partial_rows, 'seq', scatter_dimension=1, tiled=True)  20.8 us
    all_to_all x1, waiting for transfers between devices, local(): lax.all_to_all(q_buf, 'seq', split_axis=0, concat_axis=0, tiled=True)  20 us
    unnamed x15, local copies, waits for them, and re-layouts  10.3 us
  transfers between devices with their start and end apart: 6, of which 4 were waited for; matrix products, arithmetic and copies ran while one was open for 6% of the time, Pallas kernels for 0%

commit v1 on v0

v1 whole, which is shorter than its diff:
```python
import functools
import math

import jax
import jax.numpy as jnp
from jax import lax
from jax.experimental import pallas as pl
from jax.experimental.pallas import tpu as pltpu
from jax.sharding import PartitionSpec as P

MESH = pl.DeviceIdType.MESH
NX, NY, NZ = 4, 4, 8
NSEQ = 8
BLOCK = 64
F32, BF16, I32 = jnp.float32, jnp.bfloat16, jnp.int32
PEERS = ((2, 0), (2, 1), (1, 0), (1, 1), (3, 0), (3, 1), (0, 1))
DXS = (2, 1, 3)
DYS = (2, 1, 3)


def dot(a, b):
    return lax.dot_general(a, b, (((1,), (0,)), ((), ())), preferred_element_type=F32)


def dot_nt(a, b):
    return lax.dot_general(a, b, (((1,), (1,)), ((), ())), preferred_element_type=F32)


def dot_tn(a, b):
    return lax.dot_general(a, b, (((0,), (0,)), ((), ())), preferred_element_type=F32)


def iota(shape, dim):
    return lax.broadcasted_iota(I32, shape, dim)


def kernel(
    words_h, patches_h, proj_h, routes_r, targets_r, counts_s, flags_r,
    loss_o, grad_o,
    words_v, patches_v, proj_v, send_v, recv_v, meta_v, code_v, val_v,
    grad_v, dq_v, q_v, loss_s, loss_r,
    pair_s, pair_r, sum_v, a_s, a_r, b_s, b_r, a2_s, a2_r, b2_s, b2_r, z3_f, z3_s, z3_r,
    loc_sem, disp_ss, disp_rs, meta_ss, meta_rs, agz_ss, agz_rs, agx_ss, agx_rs, sib_ss, sib_rs,
    loss_ss, loss_rs, pair_ss, pair_rs, a_ss, a_rs, b_ss, b_rs, a2_ss, a2_rs, b2_ss, b2_rs, z3_ss, z3_rs,
):
    pages, wdev, width = words_v.shape
    ppsz = patches_v.shape[1]
    cap = 2 * wdev // NSEQ
    scale = 2.0 / math.sqrt(width)
    d = lax.axis_index("dp")
    s = lax.axis_index("seq")
    x, z = d // NZ, d % NZ
    y, c = s // 2, s % 2

    def seq_of(dy, dc):
        return ((y + dy) % NY) * 2 + (c + dc) % 2

    def to_seq(dy, dc):
        return {"dp": d, "seq": seq_of(dy, dc)}

    def to_x(dx):
        return {"dp": ((x + dx) % NX) * NZ + z, "seq": s}

    def to_z(dz):
        return {"dp": x * NZ + (z + dz) % NZ, "seq": s}

    def remote(src, dst, ss, rs, dev):
        return pltpu.make_async_remote_copy(
            src_ref=src, dst_ref=dst, send_sem=ss, recv_sem=rs, device_id=dev, device_id_type=MESH
        )

    sent = []

    def go(cp):
        cp.start()
        sent.append(cp)
        return cp

    rows = proj_h.shape[0]
    loads = [
        pltpu.make_async_copy(words_h.at[p], words_v.at[p], loc_sem.at[p]) for p in range(pages)
    ]
    for k in range(2):
        cols = pl.ds(pl.multiple_of((2 * c + k) * 256, 256), 256)
        loads.append(
            pltpu.make_async_copy(
                proj_h.at[:, cols],
                proj_v.at[2 * c + k, pl.ds(pl.multiple_of(d * rows, rows), rows)],
                loc_sem.at[pages + k],
            )
        )
    loads.append(pltpu.make_async_copy(patches_h, patches_v, loc_sem.at[pages + 2]))
    for cp in loads:
        cp.start()

    barrier = pltpu.get_barrier_semaphore()
    greet = [to_seq(*t) for t in PEERS] + [to_x(i) for i in DXS] + [to_z(i) for i in range(1, NZ)]
    for dev in greet:
        pl.semaphore_signal(barrier, inc=1, device_id=dev, device_id_type=MESH)

    routes = routes_r[...]
    meta_v[s, 0:pages, :] = routes
    meta_v[s, pages : 2 * pages, :] = targets_r[...]
    upper = (iota((wdev, wdev), 0) < iota((wdev, wdev), 1)).astype(BF16)
    for p in range(pages):
        route = jnp.broadcast_to(routes[p : p + 1, :], (NSEQ, wdev))
        hot = route == iota((NSEQ, wdev), 0)
        rank = dot(hot.astype(BF16), upper)
        slot = jnp.sum(jnp.where(hot, rank, 0.0), axis=0, keepdims=True).astype(I32)
        code = routes[p : p + 1, :] * cap + slot
        pick = (jnp.broadcast_to(code, (NSEQ * cap, wdev)) == iota((NSEQ * cap, wdev), 0)).astype(F32).astype(BF16)
        loads[p].wait()
        buf = dot(pick, words_v[p]).astype(BF16)
        send_v[p] = buf.reshape(NSEQ, cap, width)
        recv_v[p, s] = send_v[p, s]

    pl.semaphore_wait(barrier, len(greet))

    def dispatch(p, i):
        dy, dc = PEERS[i]
        return remote(
            send_v.at[p, seq_of(dy, dc)], recv_v.at[p, s], disp_ss.at[p, i], disp_rs.at[p, i], to_seq(dy, dc)
        )

    def send_page(p):
        for i in range(len(PEERS)):
            go(dispatch(p, i))

    def ag_z(k, i):
        own = proj_v.at[2 * c + k, pl.ds(pl.multiple_of(d * rows, rows), rows)]
        return remote(own, own, agz_ss.at[k, i - 1], agz_rs.at[k, i - 1], to_z(i))

    xrows = width // NX

    def pblock(k, xb, lo, n):
        return proj_v.at[2 * c + k, pl.ds(pl.multiple_of(xb * xrows + lo, 128), n)]

    def ag_x(k, hop):
        half = xrows // 2
        ref, dx = (
            (pblock(k, x, 0, xrows), 1),
            (pblock(k, x, 0, xrows), 3),
            (pblock(k, (x + 3) % NX, 0, half), 1),
            (pblock(k, (x + 1) % NX, half, half), 3),
        )[hop]
        return remote(ref, ref, agx_ss.at[k, hop], agx_rs.at[k, hop], to_x(dx))

    def ag_sib(k, dx):
        ref = pblock(k, (x + dx) % NX, 0, xrows)
        return remote(ref, ref, sib_ss.at[k, dx], sib_rs.at[k, dx], to_seq(0, 1))

    send_page(0)
    for k in range(2):
        loads[pages + k].wait()
        for i in range(1, NZ):
            go(ag_z(k, i))
    meta_cp = []
    for i, (dy, dc) in enumerate(PEERS):
        meta_cp.append(go(remote(meta_v.at[s], meta_v.at[s], meta_ss.at[i], meta_rs.at[i], to_seq(dy, dc))))
    for p in range(1, pages):
        send_page(p)

    grad_v[...] = jnp.zeros_like(grad_v)

    for k in range(2):
        for i in range(1, NZ):
            ag_z(k, i).wait_recv()
        go(ag_x(k, 0))
        go(ag_x(k, 1))
        go(ag_sib(k, 0))

    for cp in meta_cp:
        cp.wait_recv()
    for h in range(NSEQ):
        here = meta_v[h, 0:pages, :] == s
        rank = dot(here.astype(F32).astype(BF16), upper)
        code_v[h] = jnp.where(here, rank.astype(I32), -1)
        val_v[h] = (meta_v[h, pages : 2 * pages, :] + iota((pages, wdev), 1) * ppsz + 1).astype(F32)

    for k in range(2):
        ag_x(k, 0).wait_recv()
        ag_x(k, 1).wait_recv()
        go(ag_x(k, 2))
        go(ag_x(k, 3))
        go(ag_sib(k, 1))
        go(ag_sib(k, 3))
    for k in range(2):
        ag_x(k, 2).wait_recv()
        ag_x(k, 3).wait_recv()
        go(ag_sib(k, 2))
    loads[pages + 2].wait()
    for k in range(2):
        for dx in range(NX):
            ag_sib(k, dx).wait_recv()

    n_slots = NSEQ * cap
    spread = (iota((4 * NSEQ, ppsz), 0) == s * (ppsz // BLOCK) + iota((4 * NSEQ, ppsz), 1) // BLOCK).astype(F32).astype(BF16)
    home = iota((n_slots, 1), 0) // cap
    cand = iota((n_slots, ppsz), 1)

    def front(p):
        for i in range(len(PEERS)):
            dispatch(p, i).wait_recv()
        got = recv_v[p].reshape(n_slots, width)
        for k in range(4):
            q_v[:, k * 256 : (k + 1) * 256] = dot(got, proj_v[k]).astype(BF16)
        scores = dot_nt(q_v[...], patches_v[p]) * scale
        own = [
            jnp.broadcast_to(code_v[h, pl.ds(p, 1), :], (cap, wdev)) == iota((cap, wdev), 0) for h in range(NSEQ)
        ]
        val = jnp.concatenate(
            [
                jnp.sum(jnp.where(own[h], jnp.broadcast_to(val_v[h, pl.ds(p, 1), :], (cap, wdev)), 0.0), axis=1, keepdims=True)
                for h in range(NSEQ)
            ],
            axis=0,
        ).astype(I32)
        packed = jnp.maximum(val - 1, 0)
        tgt = packed % ppsz
        word = home * wdev + packed // ppsz
        hit = dot(
            (word // BLOCK == iota((n_slots, 2 * NSEQ), 1)).astype(F32).astype(BF16),
            dot(flags_r[p].astype(F32).astype(BF16), spread).astype(BF16),
        )
        allowed = (hit > 0.0) | (tgt // BLOCK == cand // BLOCK)
        expo = jnp.where(allowed, jnp.exp(scores), 0.0)
        total = jnp.sum(expo, axis=1, keepdims=True)
        is_t = cand == tgt
        t_score = jnp.sum(jnp.where(is_t, scores, 0.0), axis=1, keepdims=True)
        count = counts_s[p]
        valid = (val > 0) & (word < count)
        loss = jnp.where(valid, jnp.log(total) - t_score, 0.0)
        coef = jnp.where(valid, 64.0 / jnp.full((n_slots, 1), count, I32).astype(F32), 0.0)
        dscore = (coef * (expo * (1.0 / total) - jnp.where(is_t, 1.0, 0.0))).astype(BF16)
        dq = (dot(dscore, patches_v[p]) * scale).astype(BF16)
        for j in range(NSEQ):
            at = ((j + c) % 2) * (width // 2) + (j // 2) * 128
            dq_v[:, pl.ds(pl.multiple_of(at, 128), 128)] = dq[:, j * 128 : (j + 1) * 128]
        for h in range(NSEQ):
            loss_s[h, pl.ds(p, 1), :] = jnp.sum(
                jnp.where(own[h], jnp.broadcast_to(loss[h * cap : (h + 1) * cap], (cap, wdev)), 0.0),
                axis=0,
                keepdims=True,
            )

    def page(p, carry):
        front(p)
        for r in range(4):
            grad_v[r * 256 : (r + 1) * 256, :] += dot_tn(
                recv_v[p, :, :, r * 256 : (r + 1) * 256].reshape(n_slots, 256), dq_v[...]
            )
        return carry

    lax.fori_loop(0, pages - 1, page, 0)
    last = pages - 1
    front(last)

    loss_cp = []
    for i, (dy, dc) in enumerate(PEERS):
        loss_cp.append(
            go(remote(loss_s.at[seq_of(dy, dc)], loss_r.at[i], loss_ss.at[i], loss_rs.at[i], to_seq(dy, dc)))
        )

    half = width // 2
    order = [(x + i) % NX for i in DXS] + [x]
    pair_cp = []
    for i, xb in enumerate(order):
        at = pl.ds(pl.multiple_of(xb * 256, 256), 256)
        g = grad_v[at, :] + dot_tn(recv_v[last, :, :, at].reshape(n_slots, 256), dq_v[...])
        pair_s[i] = g[:, half:].astype(BF16)
        pair_cp.append(go(remote(pair_s.at[i], pair_r.at[i], pair_ss.at[i], pair_rs.at[i], to_seq(0, 1))))
        sum_v[i] = g[:, :half]

    def ycols(dy):
        return pl.ds(pl.multiple_of(((y + dy) % NY) * 128, 128), 128)

    a_cp, b_cp = [], []
    for i in range(NX):
        pair_cp[i].wait_recv()
        t = (sum_v[i] + pair_r[i].astype(F32)).reshape(NZ, 2, 16, half)
        sum_v[i] = t.reshape(256, half)
        if i < 3:
            a_s[i] = t[:, 0].astype(BF16)
            a_cp.append(go(remote(a_s.at[i], a_r.at[i], a_ss.at[i], a_rs.at[i], to_x(DXS[i]))))
        for j in range(3):
            b_s[j, i] = sum_v[i, :, ycols(DYS[j])].reshape(NZ, 2, 16, 128)[:, 1].astype(BF16)
            b_cp.append(go(remote(b_s.at[j, i], b_r.at[j, i], b_ss.at[j, i], b_rs.at[j, i], to_seq(DYS[j], 0))))
    for cp in a_cp:
        cp.wait_recv()
    t = sum_v[3].reshape(NZ, 2, 16, half)
    acc = t[:, 0]
    for i in range(3):
        acc = acc + a_r[i].astype(F32)
    sum_v[3] = jnp.concatenate([acc[:, None], t[:, 1:2]], axis=1).reshape(256, half)
    a2_cp, b2_cp = [], []
    for j in range(3):
        a2_s[j] = sum_v[3, :, ycols(DYS[j])].reshape(NZ, 2, 16, 128)[:, 0].astype(BF16)
        a2_cp.append(go(remote(a2_s.at[j], a2_r.at[j], a2_ss.at[j], a2_rs.at[j], to_seq(DYS[j], 0))))
    for cp in b_cp:
        cp.wait_recv()
    for i in range(NX):
        acc = sum_v[i, :, ycols(0)].reshape(NZ, 2, 16, 128)[:, 1]
        for j in range(3):
            acc = acc + b_r[j, i].astype(F32)
        if i < 3:
            b2_s[i] = acc.astype(BF16)
            b2_cp.append(go(remote(b2_s.at[i], b2_r.at[i], b2_ss.at[i], b2_rs.at[i], to_x(DXS[i]))))
    acc_b = acc
    acc_a = sum_v[3, :, ycols(0)].reshape(NZ, 2, 16, 128)[:, 0]
    for cp in a2_cp + b2_cp:
        cp.wait_recv()
    for j in range(3):
        acc_a = acc_a + a2_r[j].astype(F32)
        acc_b = acc_b + b2_r[j].astype(F32)
    z3_f[:, 0:16, :] = acc_a
    z3_f[:, 16:32, :] = acc_b
    z3_s[...] = z3_f[...].astype(BF16)
    z3_cp = []
    for i in range(1, NZ):
        z3_cp.append(go(remote(z3_s.at[(z + i) % NZ], z3_r.at[i - 1], z3_ss.at[i - 1], z3_rs.at[i - 1], to_z(i))))
    for cp in loss_cp:
        cp.wait_recv()
    loss_o[...] = loss_s[s] + jnp.sum(loss_r[...], axis=0)
    for cp in z3_cp:
        cp.wait_recv()
    grad_o[...] = z3_f[z] + jnp.sum(z3_r[...].astype(F32), axis=0)
    for cp in sent:
        cp.wait_send()


def local(words, patches, proj, routes, targets, counts, flags):
    pages, wdev, width = words.shape
    ppsz = patches.shape[1]
    cap = 2 * wdev // NSEQ
    half = width // 2
    vm = pltpu.VMEM
    dma = pltpu.SemaphoreType.DMA
    any_ = pl.BlockSpec(memory_space=pl.ANY)
    vmem = pl.BlockSpec(memory_space=pltpu.VMEM)
    pairs = [(pages, 7), (7,), (2, 7), (2, 4), (2, 4), (7,), (4,), (3,), (3, 4), (3,), (3,), (7,)]
    loss, grad = pl.pallas_call(
        kernel,
        out_shape=(
            jax.ShapeDtypeStruct((pages, wdev), F32),
            jax.ShapeDtypeStruct((width // (NX * NZ), width // NSEQ), F32),
        ),
        in_specs=[any_, any_, any_, vmem, vmem, pl.BlockSpec(memory_space=pltpu.SMEM), vmem],
        out_specs=(vmem, vmem),
        scratch_shapes=[
            vm((pages, wdev, width), BF16),
            vm((pages, ppsz, width), BF16),
            vm((4, width, 256), BF16),
            vm((pages, NSEQ, cap, width), BF16),
            vm((pages, NSEQ, cap, width), BF16),
            vm((NSEQ, 2 * pages, wdev), I32),
            vm((NSEQ, pages, wdev), I32),
            vm((NSEQ, pages, wdev), F32),
            vm((width, width), F32),
            vm((NSEQ * cap, width), BF16),
            vm((NSEQ * cap, width), BF16),
            vm((NSEQ, pages, wdev), F32),
            vm((7, pages, wdev), F32),
            vm((NX, 256, half), BF16),
            vm((NX, 256, half), BF16),
            vm((NX, 256, half), F32),
            vm((3, NZ, 16, half), BF16),
            vm((3, NZ, 16, half), BF16),
            vm((3, NX, NZ, 16, 128), BF16),
            vm((3, NX, NZ, 16, 128), BF16),
            vm((3, NZ, 16, 128), BF16),
            vm((3, NZ, 16, 128), BF16),
            vm((3, NZ, 16, 128), BF16),
            vm((3, NZ, 16, 128), BF16),
            vm((NZ, 32, 128), F32),
            vm((NZ, 32, 128), BF16),
            vm((7, 32, 128), BF16),
            dma((pages + 3,)),
        ]
        + [dma(shape) for shape in pairs for _ in range(2)],
        compiler_params=pltpu.CompilerParams(collective_id=1, has_side_effects=True, vmem_limit_bytes=56 << 20),
        name="grounding",
    )(words, patches, proj, routes.reshape(pages, wdev), targets, counts, flags)
    return loss, grad


def solution(mesh):
    in_specs = (
        P("dp", "seq", None),
        P("dp", "seq", None),
        P("dp", None),
        P("dp", "seq", None),
        P("dp", "seq"),
        P("dp"),
        P("dp", None, None),
    )
    out_specs = (P("dp", "seq"), P("dp", "seq"))
    return jax.shard_map(local, mesh=mesh, in_specs=in_specs, out_specs=out_specs, check_vma=False)
```

time: 442 us -> 63.4 us (0.14)
  waiting for transfers between devices: 327 us -> 0 us
  Pallas kernels: 0 us -> 59.2 us
  blocking collectives: 38.6 us -> 0 us
  matrix products: 24.8 us -> 0 us
  starting transfers between devices: 16.3 us -> 0 us
  between operations: 13.9 us -> 0.64 us
  local copies, waits for them, and re-layouts: 13.6 us -> 2.55 us
    unnamed x4 -> x0, waiting for transfers between devices: 219 us -> none
    all_gather x1 -> x0, waiting for transfers between devices: 66.9 us -> none  [local(): lax.all_gather(proj, 'dp', axis=0, tiled=True)]
    pallas_call x0 -> x1, Pallas kernels: none -> 59.2 us  [local(): pl.pallas_call(kernel, out_shape=(jax.ShapeDtypeStruct((pages, wdev), F32...]
    all_to_all x2 -> x0, blocking collectives: 38.6 us -> none  [the longest x1 30.8 us: local(): lax.all_to_all(dquery, 'seq', split_axis=0, concat_axis=0, tiled=True)]
    dot_general x8 -> x0, matrix products: 24.8 us -> none  [the longest x1 5.12 us: local(): jnp.einsum('rc,rd->cd', columns, right, preferred_element_type=jnp.float32)]
    reduce_scatter x1 -> x0, waiting for transfers between devices: 20.8 us -> none  [local(): lax.psum_scatter(partial_rows, 'seq', scatter_dimension=1, tiled=True)]
    all_to_all x3 -> x0, waiting for transfers between devices: 20 us -> none  [the longest x1 20 us: local(): lax.all_to_all(q_buf, 'seq', split_axis=0, concat_axis=0, tiled=True)]
    all_to_all x3 -> x0, starting transfers between devices: 16.2 us -> none  [the longest x1 6.25 us: local(): lax.all_to_all(q_buf, 'seq', split_axis=0, concat_axis=0, tiled=True)]
  transfers between devices with their start and end apart: 6 -> 0, of which waited for: 4 -> 0; matrix products, arithmetic and copies ran while one was open for 6% -> 0% of each run, Pallas kernels for 0% -> 0%
where the time goes in v1:
time: 63.4 us; the launch traced here: 62.4 us
  Pallas kernels  59.2 us (93%)
  local copies, waits for them, and re-layouts  2.55 us (4%)
  between operations  0.64 us (1%)
    pallas_call x1, Pallas kernels, local(): pl.pallas_call(kernel, out_shape=(jax.ShapeDtypeStruct((pages, wdev), F32...  59.2 us
    unnamed x2, local copies, waits for them, and re-layouts  2.55 us

profile of v1, /device:TPU:24, one launch (start us, length us, event | category | flops | bytes accessed | tf_op | source)
XLA Modules:
  0.0 62.4 jit_solution(111909399335030831)
XLA Ops:
  0.6 59.2 %grounding.1 = (f32[4,128]{1,0:T(4,128)}, f32[32,128]{1,0:T(8,128)}) custom-call(bf16[4,128,1024]{2,1,0:T(8,128)(2,1)} %words_h.1, bf16[4,256,1024]{2,1,0:T(8,128)(2,1)} %patches_h.1, bf16[32,1024]{1,0:T(8,128)(2,1)} %proj_h.1, s32[4,128]{1,0:T(4,128)} %bitcast.1, s32[4,128]{1,0:T(4,128)} %targets_r.1, s32[4]{0:T(128)} %counts_s.1, s32[4,16,32]{2,1,0:T(8,128)} %flags_r.1), custom_call_target="tpu_custom_call" | custom-call | tf_op jit(solution)/shard_map/grounding/pallas_call | solution.py:341
  59.8 1.2 %copy.11 = f32[4,128]{1,0:T(4,128)} copy(f32[4,128]{1,0:T(4,128)} %get-tuple-element.4) | data formatting | bytes 4096
  61.1 1.3 %copy.12 = f32[32,128]{1,0:T(8,128)} copy(f32[32,128]{1,0:T(8,128)} %get-tuple-element.5) | data formatting | bytes 32768

commit v2 on v1

v2 whole, which is shorter than its diff:
```python
import functools
import math

import jax
import jax.numpy as jnp
from jax import lax
from jax.experimental import pallas as pl
from jax.experimental.pallas import tpu as pltpu
from jax.sharding import PartitionSpec as P

MESH = pl.DeviceIdType.MESH
NX, NY, NZ = 4, 4, 8
NSEQ = 8
BLOCK = 64
F32, BF16, I32 = jnp.float32, jnp.bfloat16, jnp.int32
PEERS = ((2, 0), (2, 1), (1, 0), (1, 1), (3, 0), (3, 1), (0, 1))
DXS = (2, 1, 3)
DYS = (2, 1, 3)
ZORDER = (4, 3, 5, 2, 6, 1, 7)


def dot(a, b):
    return lax.dot_general(a, b, (((1,), (0,)), ((), ())), preferred_element_type=F32)


def dot_nt(a, b):
    return lax.dot_general(a, b, (((1,), (1,)), ((), ())), preferred_element_type=F32)


def dot_tn(a, b):
    return lax.dot_general(a, b, (((0,), (0,)), ((), ())), preferred_element_type=F32)


def iota(shape, dim):
    return lax.broadcasted_iota(I32, shape, dim)


def kernel(
    words_h, patches_h, proj_h, routes_h, targets_h, counts_h, flags_h,
    loss_o, grad_o,
    routes_r, targets_r, counts_s, flags_r, words_v, patches_v, proj_v, send_v, recv_v, meta_v, code_v, val_v,
    grad_v, mask_v, tgt_v, coef_v, loss_v, dq_v, q_v, loss_s, loss_r,
    pair_s, pair_r, sum_v, a_s, a_r, ar_r, a_f, b_s, b_r, br_r, a2_s, a2_r, b2_s, b2_r, z3_f, z3_s, z3_r,
    loc_sem, disp_ss, disp_rs, meta_ss, meta_rs, aga_ss, aga_rs, agb_ss, agb_rs, sib_ss, sib_rs,
    loss_ss, loss_rs, pair_ss, pair_rs, a_ss, a_rs, ar_ss, ar_rs, b_ss, b_rs, br_ss, br_rs, a2_ss, a2_rs, b2_ss, b2_rs, z3_ss, z3_rs,
):
    pages, wdev, width = words_v.shape
    ppsz = patches_v.shape[1]
    cap = 2 * wdev // NSEQ
    scale = 2.0 / math.sqrt(width)
    d = lax.axis_index("dp")
    s = lax.axis_index("seq")
    x, z = d // NZ, d % NZ
    y, c = s // 2, s % 2

    def seq_of(dy, dc):
        return ((y + dy) % NY) * 2 + (c + dc) % 2

    def to_seq(dy, dc):
        return {"dp": d, "seq": seq_of(dy, dc)}

    def to_x(dx):
        return {"dp": ((x + dx) % NX) * NZ + z, "seq": s}

    def to_z(dz):
        return {"dp": x * NZ + (z + dz) % NZ, "seq": s}

    def remote(src, dst, ss, rs, dev):
        return pltpu.make_async_remote_copy(
            src_ref=src, dst_ref=dst, send_sem=ss, recv_sem=rs, device_id=dev, device_id_type=MESH
        )

    sent = []

    def go(cp):
        cp.start()
        sent.append(cp)
        return cp

    barrier = pltpu.get_barrier_semaphore()
    greet = [to_seq(*t) for t in PEERS] + [to_x(i) for i in DXS] + [to_z(i) for i in range(1, NZ)]
    for dev in greet:
        pl.semaphore_signal(barrier, inc=1, device_id=dev, device_id_type=MESH)

    rows = proj_h.shape[0]
    loads = [
        pltpu.make_async_copy(words_h.at[p], words_v.at[p], loc_sem.at[p]) for p in range(pages)
    ]
    for k in range(2):
        cols = pl.ds(pl.multiple_of((2 * c + k) * 256, 256), 256)
        loads.append(
            pltpu.make_async_copy(
                proj_h.at[:, cols],
                proj_v.at[2 * c + k, x, pl.ds(pl.multiple_of(z * rows, rows), rows)],
                loc_sem.at[pages + k],
            )
        )
    loads.append(pltpu.make_async_copy(patches_h, patches_v, loc_sem.at[pages + 2]))
    small = [
        pltpu.make_async_copy(src, dst, loc_sem.at[pages + 3 + i])
        for i, (src, dst) in enumerate(
            ((routes_h, routes_r), (targets_h, targets_r), (counts_h, counts_s), (flags_h, flags_r))
        )
    ]
    for cp in small + loads:
        cp.start()
    for cp in small:
        cp.wait()

    routes = routes_r[...]
    meta_v[s, 0:pages, :] = routes
    meta_v[s, pages : 2 * pages, :] = targets_r[...]
    upper = (iota((wdev, wdev), 0) < iota((wdev, wdev), 1)).astype(BF16)
    lanes = jnp.concatenate([jnp.broadcast_to(routes[p : p + 1, :], (NSEQ, wdev)) for p in range(pages)], axis=0)
    hot = lanes == iota((pages * NSEQ, wdev), 0) % NSEQ
    rank = jnp.where(hot, dot(hot.astype(F32).astype(BF16), upper), 0.0)

    def build(p):
        slot = jnp.sum(rank[p * NSEQ : (p + 1) * NSEQ], axis=0, keepdims=True).astype(I32)
        code = routes[p : p + 1, :] * cap + slot
        pick = (jnp.broadcast_to(code, (NSEQ * cap, wdev)) == iota((NSEQ * cap, wdev), 0)).astype(F32).astype(BF16)
        loads[p].wait()
        send_v[p] = dot(pick, words_v[p]).astype(BF16).reshape(NSEQ, cap, width)

    build(0)
    pl.semaphore_wait(barrier, len(greet))

    def dispatch(p, i):
        dy, dc = PEERS[i]
        return remote(
            send_v.at[p, seq_of(dy, dc)], recv_v.at[p, s], disp_ss.at[p, i], disp_rs.at[p, i], to_seq(dy, dc)
        )

    def send_page(p):
        for i in range(len(PEERS)):
            go(dispatch(p, i))

    def zrows(zb):
        return pl.ds(pl.multiple_of(zb * rows, rows), rows)

    half = rows * NZ // 2

    def ag_a(hop, i=0):
        if hop == 0:
            ref, dev = proj_v.at[2 * c, x, zrows(z)], to_z(i)
        elif hop == 1:
            ref, dev = proj_v.at[2 * c, x], to_x((1, 3)[i])
        else:
            ref, dev = proj_v.at[2 * c, (x + (3, 1)[i]) % NX, i * half : (i + 1) * half], to_x((1, 3)[i])
        at = i - 1 if hop == 0 else NZ - 1 + 2 * (hop - 1) + i
        return remote(ref, ref, aga_ss.at[at], aga_rs.at[at], dev)

    def ag_b(hop, i):
        if hop == 0:
            ref, dev = proj_v.at[2 * c + 1, x, zrows(z)], to_x(DXS[i])
        else:
            ref, dev = proj_v.at[2 * c + 1, :, zrows(z)], to_z(i)
        at = i if hop == 0 else 2 + i
        return remote(ref, ref, agb_ss.at[at], agb_rs.at[at], dev)

    def sib_a(dx):
        ref = proj_v.at[2 * c, (x + dx) % NX]
        return remote(ref, ref, sib_ss.at[dx], sib_rs.at[dx], to_seq(0, 1))

    def sib_b(i):
        ref = proj_v.at[2 * c + 1, :, zrows((z + i) % NZ)]
        return remote(ref, ref, sib_ss.at[NX + i], sib_rs.at[NX + i], to_seq(0, 1))

    meta_cp = []
    for i, (dy, dc) in enumerate(PEERS):
        meta_cp.append(go(remote(meta_v.at[s], meta_v.at[s], meta_ss.at[i], meta_rs.at[i], to_seq(dy, dc))))
    send_page(0)
    for i in range(2):
        loads[pages + i].wait()
    for i in range(3):
        go(ag_b(0, i))
    for i in range(1, NZ):
        go(ag_a(0, i))
    build(1)
    send_page(1)
    build(2)
    send_page(2)
    for i in range(3):
        ag_b(0, i).wait_recv()
    for i in ZORDER:
        go(ag_b(1, i))
    go(sib_b(0))
    build(3)
    send_page(3)
    for p in range(pages):
        recv_v[p, s] = send_v[p, s]
    for i in range(1, NZ):
        ag_a(0, i).wait_recv()
    for i in range(2):
        go(ag_a(1, i))
    go(sib_a(0))

    for cp in meta_cp:
        cp.wait_recv()
    for h in range(NSEQ):
        here = meta_v[h, 0:pages, :] == s
        rank = dot(here.astype(F32).astype(BF16), upper)
        code_v[h] = jnp.where(here, rank.astype(I32), -1)
        val_v[h] = (meta_v[h, pages : 2 * pages, :] + iota((pages, wdev), 1) * ppsz + 1).astype(F32)

    n_slots = NSEQ * cap
    spread = (iota((4 * NSEQ, ppsz), 0) == s * (ppsz // BLOCK) + iota((4 * NSEQ, ppsz), 1) // BLOCK).astype(F32).astype(BF16)
    home = iota((n_slots, 1), 0) // cap
    cand = iota((n_slots, ppsz), 1)

    def owned(p):
        return [
            jnp.broadcast_to(code_v[h, pl.ds(p, 1), :], (cap, wdev)) == iota((cap, wdev), 0) for h in range(NSEQ)
        ]

    def prepare(p):
        own = owned(p)
        val = jnp.concatenate(
            [
                jnp.sum(jnp.where(own[h], jnp.broadcast_to(val_v[h, pl.ds(p, 1), :], (cap, wdev)), 0.0), axis=1, keepdims=True)
                for h in range(NSEQ)
            ],
            axis=0,
        ).astype(I32)
        packed = jnp.maximum(val - 1, 0)
        tgt = packed % ppsz
        word = home * wdev + packed // ppsz
        hit = dot(
            (word // BLOCK == iota((n_slots, 2 * NSEQ), 1)).astype(F32).astype(BF16),
            dot(flags_r[p].astype(F32).astype(BF16), spread).astype(BF16),
        )
        allowed = (hit > 0.0) | (tgt // BLOCK == cand // BLOCK)
        mask_v[p] = allowed.astype(F32).astype(BF16)
        tgt_v[p] = tgt
        count = counts_s[p]
        valid = (val > 0) & (word < count)
        coef_v[p] = jnp.where(valid, 64.0 / jnp.full((n_slots, 1), count, I32).astype(F32), 0.0)

    for p in range(2):
        prepare(p)
    for i in range(2):
        ag_a(1, i).wait_recv()
    for i in range(2):
        go(ag_a(2, i))
    go(sib_a(1))
    go(sib_a(3))
    for p in range(2, pages):
        prepare(p)
    for i in ZORDER:
        ag_b(1, i).wait_recv()
        go(sib_b(NZ - i))
    for i in range(2):
        ag_a(2, i).wait_recv()
    go(sib_a(2))
    loads[pages + 2].wait()
    for i in range(NZ):
        sib_b(i).wait_recv()
    for i in range(NX):
        sib_a(i).wait_recv()

    def front(p):
        for i in range(len(PEERS)):
            dispatch(p, i).wait_recv()
        got = recv_v[p].reshape(n_slots, width)
        for k in range(4):
            q_v[:, k * 256 : (k + 1) * 256] = dot(got, proj_v[k].reshape(width, 256)).astype(BF16)
        scores = dot_nt(q_v[...], patches_v[p]) * scale
        expo = jnp.where(mask_v[p].astype(F32) > 0.0, jnp.exp(scores), 0.0)
        total = jnp.sum(expo, axis=1, keepdims=True)
        is_t = cand == tgt_v[p]
        t_score = jnp.sum(jnp.where(is_t, scores, 0.0), axis=1, keepdims=True)
        coef = coef_v[p]
        loss_v[p] = jnp.where(coef > 0.0, jnp.log(total) - t_score, 0.0)
        dscore = (coef * (expo * (1.0 / total) - jnp.where(is_t, 1.0, 0.0))).astype(BF16)
        dq = (dot(dscore, patches_v[p]) * scale).astype(BF16)
        for j in range(NSEQ):
            at = ((j + c) % 2) * (width // 2) + (j // 2) * 128
            dq_v[p, :, pl.ds(pl.multiple_of(at, 128), 128)] = dq[:, j * 128 : (j + 1) * 128]

    def send_home(p):
        own, loss = owned(p), loss_v[p]
        for h in range(NSEQ):
            loss_s[h, pl.ds(p, 1), :] = jnp.sum(
                jnp.where(own[h], jnp.broadcast_to(loss[h * cap : (h + 1) * cap], (cap, wdev)), 0.0),
                axis=0,
                keepdims=True,
            )

    def page(p, carry):
        front(p)
        send_home(p)
        return carry

    last = pages - 1
    lax.fori_loop(0, last, page, 0)
    for r in range(4):
        grad_v[r * 256 : (r + 1) * 256, :] = dot_tn(
            recv_v[0:last, :, :, r * 256 : (r + 1) * 256].reshape(last * n_slots, 256),
            dq_v[0:last].reshape(last * n_slots, width),
        )
    front(last)

    n_early = len(sent)

    half = width // 2
    order = [(x + i) % NX for i in DXS] + [x]
    pair_cp = []
    for i, xb in enumerate(order):
        at = pl.ds(pl.multiple_of(xb * 256, 256), 256)
        g = grad_v[at, :] + dot_tn(recv_v[last, :, :, at].reshape(n_slots, 256), dq_v[last])
        pair_s[i] = g[:, half:].astype(BF16)
        pair_cp.append(go(remote(pair_s.at[i], pair_r.at[i], pair_ss.at[i], pair_rs.at[i], to_seq(0, 1))))
        sum_v[i] = g[:, :half]

    def ycols(dy):
        return pl.ds(pl.multiple_of(((y + dy) % NY) * 128, 128), 128)

    def part(i, which, cols=None):
        ref = sum_v[i] if cols is None else sum_v[i, :, cols]
        return ref.reshape(NZ, 2, 16, ref.shape[-1])[:, which]

    zh = NZ // 2
    halves = (slice(0, zh), slice(zh, NZ))
    step = (1, 3)
    ar_cp, ad_cp, br_cp, bd_cp = [None] * 2, [None] * 2, [], []
    for i in range(NX):
        pair_cp[i].wait_recv()
        sum_v[i] += pair_r[i].astype(F32)
        if i == 0:
            a_s[0] = part(0, 0).astype(BF16)
            for w in range(2):
                src = a_s.at[0, pl.ds(w * zh, zh)]
                ar_cp[w] = go(remote(src, ar_r.at[w], ar_ss.at[w], ar_rs.at[w], to_x(step[w])))
        elif i < 3:
            w = i - 1
            a_s[1 + w, halves[1 - w]] = part(i, 0)[halves[1 - w]].astype(BF16)
            at = pl.ds((1 - w) * zh, zh)
            ad_cp[w] = go(remote(a_s.at[1 + w, at], a_r.at[w, at], a_ss.at[w, 0], a_rs.at[w, 0], to_x(step[w])))
        far = part(i, 1, ycols(2)).astype(BF16)
        for w in range(2):
            b_s[w, 0, i] = far[halves[w]]
            b_s[w, 1, i] = part(i, 1, ycols(step[w]))[halves[1 - w]].astype(BF16)
            br_cp.append(go(remote(b_s.at[w, 0, i], br_r.at[w, i], br_ss.at[w, i], br_rs.at[w, i], to_seq(step[w], 0))))
            bd_cp.append(
                go(remote(b_s.at[w, 1, i], b_r.at[w, 0, i], b_ss.at[w, 0, i], b_rs.at[w, 0, i], to_seq(step[w], 0)))
            )
    am_cp, bm_cp = [], []
    for w in range(2):
        ar_cp[w].wait_recv()
        a_s[1 + w, halves[w]] = (part(1 + w, 0)[halves[w]] + ar_r[w].astype(F32)).astype(BF16)
        at = pl.ds(w * zh, zh)
        am_cp.append(go(remote(a_s.at[1 + w, at], a_r.at[w, at], a_ss.at[w, 1], a_rs.at[w, 1], to_x(step[w]))))
    for i in range(NX):
        for w in range(2):
            br_cp[2 * i + w].wait_recv()
            b_s[w, 2, i] = (part(i, 1, ycols(step[w]))[halves[w]] + br_r[w, i].astype(F32)).astype(BF16)
            bm_cp.append(
                go(remote(b_s.at[w, 2, i], b_r.at[w, 1, i], b_ss.at[w, 1, i], b_rs.at[w, 1, i], to_seq(step[w], 0)))
            )
    send_home(last)
    loss_cp = []
    for i, (dy, dc) in enumerate(PEERS):
        loss_cp.append(
            go(remote(loss_s.at[seq_of(dy, dc)], loss_r.at[i], loss_ss.at[i], loss_rs.at[i], to_seq(dy, dc)))
        )
    for cp in sent[:n_early]:
        cp.wait_send()
    for cp in ad_cp + am_cp:
        cp.wait_recv()
    a_f[...] = part(3, 0) + a_r[0].astype(F32) + a_r[1].astype(F32)
    a2_cp, b2_cp = [], []
    for j in range(3):
        a2_s[j] = a_f[:, :, ycols(DYS[j])].astype(BF16)
        a2_cp.append(go(remote(a2_s.at[j], a2_r.at[j], a2_ss.at[j], a2_rs.at[j], to_seq(DYS[j], 0))))
    for cp in bd_cp + bm_cp:
        cp.wait_recv()
    for i in range(NX):
        left = jnp.concatenate([b_r[0, 1, i], b_r[0, 0, i]], axis=0).astype(F32)
        right = jnp.concatenate([b_r[1, 0, i], b_r[1, 1, i]], axis=0).astype(F32)
        acc_b = part(i, 1, ycols(0)) + left + right
        if i < 3:
            b2_s[i] = acc_b.astype(BF16)
            b2_cp.append(go(remote(b2_s.at[i], b2_r.at[i], b2_ss.at[i], b2_rs.at[i], to_x(DXS[i]))))
    acc_a = a_f[:, :, ycols(0)]
    n_mid = len(sent)
    for cp in a2_cp + b2_cp:
        cp.wait_recv()
    for j in range(3):
        acc_a = acc_a + a2_r[j].astype(F32)
        acc_b = acc_b + b2_r[j].astype(F32)
    z3_f[:, 0:16, :] = acc_a
    z3_f[:, 16:32, :] = acc_b
    z3_s[...] = z3_f[...].astype(BF16)
    z3_cp = []
    for i in range(1, NZ):
        z3_cp.append(go(remote(z3_s.at[(z + i) % NZ], z3_r.at[i - 1], z3_ss.at[i - 1], z3_rs.at[i - 1], to_z(i))))
    for cp in loss_cp:
        cp.wait_recv()
    loss_o[...] = loss_s[s] + jnp.sum(loss_r[...], axis=0)
    for cp in sent[n_early:n_mid]:
        cp.wait_send()
    for cp in z3_cp:
        cp.wait_recv()
    grad_o[...] = z3_f[z] + jnp.sum(z3_r[...].astype(F32), axis=0)
    for cp in sent[n_mid:]:
        cp.wait_send()


def finish(loss_r, grad_r, loss_o, grad_o):
    loss_o[...] = loss_r[...]
    grad_o[...] = grad_r[...]


def local(words, patches, proj, routes, targets, counts, flags):
    pages, wdev, width = words.shape
    ppsz = patches.shape[1]
    cap = 2 * wdev // NSEQ
    half = width // 2
    vm = pltpu.VMEM
    dma = pltpu.SemaphoreType.DMA
    any_ = pl.BlockSpec(memory_space=pl.ANY)
    vmem = pl.BlockSpec(memory_space=pltpu.VMEM)
    pairs = [(pages, 7), (7,), (NZ + 3,), (NZ + 2,), (NX + NZ,), (7,), (4,), (2, 2), (2,), (2, 2, 4), (2, 4), (3,), (3,), (7,)]
    loss, grad = pl.pallas_call(
        kernel,
        out_shape=(vm((pages, wdev), F32), vm((width // (NX * NZ), width // NSEQ), F32)),
        in_specs=[any_] * 7,
        out_specs=(vmem, vmem),
        scratch_shapes=[
            vm((pages, wdev), I32),
            vm((pages, wdev), I32),
            pltpu.SMEM(counts.shape, I32),
            vm(flags.shape, I32),
            vm((pages, wdev, width), BF16),
            vm((pages, ppsz, width), BF16),
            vm((4, NX, width // NX, 256), BF16),
            vm((pages, NSEQ, cap, width), BF16),
            vm((pages, NSEQ, cap, width), BF16),
            vm((NSEQ, 2 * pages, wdev), I32),
            vm((NSEQ, pages, wdev), I32),
            vm((NSEQ, pages, wdev), F32),
            vm((width, width), F32),
            vm((pages, NSEQ * cap, ppsz), BF16),
            vm((pages, NSEQ * cap, 1), I32),
            vm((pages, NSEQ * cap, 1), F32),
            vm((pages, NSEQ * cap, 1), F32),
            vm((pages, NSEQ * cap, width), BF16),
            vm((NSEQ * cap, width), BF16),
            vm((NSEQ, pages, wdev), F32),
            vm((7, pages, wdev), F32),
            vm((NX, 256, half), BF16),
            vm((NX, 256, half), BF16),
            vm((NX, 256, half), F32),
            vm((3, NZ, 16, half), BF16),
            vm((2, NZ, 16, half), BF16),
            vm((2, NZ // 2, 16, half), BF16),
            vm((NZ, 16, half), F32),
            vm((2, 3, NX, NZ // 2, 16, 128), BF16),
            vm((2, 2, NX, NZ // 2, 16, 128), BF16),
            vm((2, NX, NZ // 2, 16, 128), BF16),
            vm((3, NZ, 16, 128), BF16),
            vm((3, NZ, 16, 128), BF16),
            vm((3, NZ, 16, 128), BF16),
            vm((3, NZ, 16, 128), BF16),
            vm((NZ, 32, 128), F32),
            vm((NZ, 32, 128), BF16),
            vm((7, 32, 128), BF16),
            dma((pages + 7,)),
        ]
        + [dma(shape) for shape in pairs for _ in range(2)],
        compiler_params=pltpu.CompilerParams(collective_id=1, has_side_effects=True, vmem_limit_bytes=56 << 20),
        name="grounding",
    )(words, patches, proj, routes.reshape(pages, wdev), targets, counts, flags)
    return pl.pallas_call(
        finish,
        out_shape=(jax.ShapeDtypeStruct(loss.shape, F32), jax.ShapeDtypeStruct(grad.shape, F32)),
        in_specs=[vmem, vmem],
        out_specs=(vmem, vmem),
        name="finish",
    )(pltpu.with_memory_space_constraint(loss, pltpu.VMEM), pltpu.with_memory_space_constraint(grad, pltpu.VMEM))


def solution(mesh):
    in_specs = (
        P("dp", "seq", None),
        P("dp", "seq", None),
        P("dp", None),
        P("dp", "seq", None),
        P("dp", "seq"),
        P("dp"),
        P("dp", None, None),
    )
    out_specs = (P("dp", "seq"), P("dp", "seq"))
    return jax.shard_map(local, mesh=mesh, in_specs=in_specs, out_specs=out_specs, check_vma=False)
```

time: 63.4 us -> 57.3 us (0.904); the launches traced: 62.4 us -> 57.2 us
  Pallas kernels: 59.2 us -> 56.6 us
  local copies, waits for them, and re-layouts: 2.55 us -> 0 us
    pallas_call x1 -> x2, Pallas kernels: 59.2 us -> 56.6 us  [the longest x1 56 us: local(): pl.pallas_call(kernel, out_shape=(vm((pages, wdev), F32), vm((width // (N...]
    unnamed x2 -> x0, local copies, waits for them, and re-layouts: 2.55 us -> none
where the time goes in v2:
time: 57.3 us; the launch traced here: 57.2 us
  Pallas kernels  56.6 us (99%)
  between operations  0.64 us (1%)
    pallas_call x1, Pallas kernels, local(): pl.pallas_call(kernel, out_shape=(vm((pages, wdev), F32), vm((width // (N...  56 us

profile of v2, /device:TPU:24, one launch (start us, length us, event | category | flops | bytes accessed | tf_op | source)
XLA Modules:
  0.0 57.2 jit_solution(15328925788505485843)
XLA Ops:
  0.6 56.0 %grounding.1 = (f32[4,128]{1,0:T(4,128)S(1)}, f32[32,128]{1,0:T(8,128)S(1)}) custom-call(bf16[4,128,1024]{2,1,0:T(8,128)(2,1)} %words_h.1, bf16[4,256,1024]{2,1,0:T(8,128)(2,1)} %patches_h.1, bf16[32,1024]{1,0:T(8,128)(2,1)} %proj_h.1, s32[4,128]{1,0:T(4,128)} %bitcast.1, s32[4,128]{1,0:T(4,128)} %targets_h.1, s32[4]{0:T(128)} %counts_h.1, s32[4,16,32]{2,1,0:T(8,128)} %flags_h.1), custom_call_target="tpu_custom_call" | custom-call | tf_op jit(solution)/shard_map/grounding/pallas_call | solution.py:424
  56.6 0.6 %finish.1 = (f32[4,128]{1,0:T(4,128)}, f32[32,128]{1,0:T(8,128)}) custom-call(f32[4,128]{1,0:T(4,128)S(1)} %get-tuple-element.4.loss_r, f32[32,128]{1,0:T(8,128)S(1)} %get-tuple-element.5.grad_r), custom_call_target="tpu_custom_call" | custom-call | tf_op jit(solution)/shard_map/finish/pallas_call | solution.py:474

commit v3 on v2

--- a/solution.py
+++ b/solution.py
@@ -17,6 +17,7 @@
 DXS = (2, 1, 3)
 DYS = (2, 1, 3)
 ZORDER = (4, 3, 5, 2, 6, 1, 7)
+ZFAR = (4, 3, 5, 2, 6, 1, 7, 0)
 
 
 def dot(a, b):
@@ -39,8 +40,8 @@
     words_h, patches_h, proj_h, routes_h, targets_h, counts_h, flags_h,
     loss_o, grad_o,
     routes_r, targets_r, counts_s, flags_r, words_v, patches_v, proj_v, send_v, recv_v, meta_v, code_v, val_v,
-    grad_v, mask_v, tgt_v, coef_v, loss_v, dq_v, q_v, loss_s, loss_r,
-    pair_s, pair_r, sum_v, a_s, a_r, ar_r, a_f, b_s, b_r, br_r, a2_s, a2_r, b2_s, b2_r, z3_f, z3_s, z3_r,
+    turned_v, grad_v, mask_v, tgt_v, coef_v, loss_v, dq_v, q_v, loss_s, loss_r,
+    pair_s, pair_r, sum_v, a_s, a_r, ar_r, a_f, b_s, b_r, br_r, a2_s, a2_r, b2_s, b2_r, b_f, z3_f, z3_s, z3_r,
     loc_sem, disp_ss, disp_rs, meta_ss, meta_rs, aga_ss, aga_rs, agb_ss, agb_rs, sib_ss, sib_rs,
     loss_ss, loss_rs, pair_ss, pair_rs, a_ss, a_rs, ar_ss, ar_rs, b_ss, b_rs, br_ss, br_rs, a2_ss, a2_rs, b2_ss, b2_rs, z3_ss, z3_rs,
 ):
@@ -244,27 +245,31 @@
         go(ag_a(2, i))
     go(sib_a(1))
     go(sib_a(3))
-    for p in range(2, pages):
-        prepare(p)
     for i in ZORDER:
         ag_b(1, i).wait_recv()
         go(sib_b(NZ - i))
     for i in range(2):
         ag_a(2, i).wait_recv()
     go(sib_a(2))
+    for p in range(2, pages):
+        prepare(p)
     loads[pages + 2].wait()
     for i in range(NZ):
         sib_b(i).wait_recv()
     for i in range(NX):
         sib_a(i).wait_recv()
 
-    def front(p):
+    def front(p, ahead=False):
         for i in range(len(PEERS)):
             dispatch(p, i).wait_recv()
         got = recv_v[p].reshape(n_slots, width)
-        for k in range(4):
-            q_v[:, k * 256 : (k + 1) * 256] = dot(got, proj_v[k].reshape(width, 256)).astype(BF16)
-        scores = dot_nt(q_v[...], patches_v[p]) * scale
+        if ahead:
+            turned_v[...] = got.T
+            scores = dot_nt(got, q_v[...]) * scale
+        else:
+            for k in range(4):
+                q_v[:, k * 256 : (k + 1) * 256] = dot(got, proj_v[k].reshape(width, 256)).astype(BF16)
+            scores = dot_nt(q_v[...], patches_v[p]) * scale
         expo = jnp.where(mask_v[p].astype(F32) > 0.0, jnp.exp(scores), 0.0)
         total = jnp.sum(expo, axis=1, keepdims=True)
         is_t = cand == tgt_v[p]
@@ -293,12 +298,22 @@
 
     last = pages - 1
     lax.fori_loop(0, last, page, 0)
-    for r in range(4):
-        grad_v[r * 256 : (r + 1) * 256, :] = dot_tn(
-            recv_v[0:last, :, :, r * 256 : (r + 1) * 256].reshape(last * n_slots, 256),
-            dq_v[0:last].reshape(last * n_slots, width),
-        )
-    front(last)
+    half = width // 2
+    order = [(x + i) % NX for i in DXS] + [x]
+    ats = [pl.ds(pl.multiple_of(xb * 256, 256), 256) for xb in order]
+
+    def before(i):
+        return dot_tn(
+            recv_v[0:last, :, :, ats[i]].reshape(last * n_slots, 256), dq_v[0:last].reshape(last * n_slots, width)
+        )
+
+    for i in range(3):
+        grad_v[i * 256 : (i + 1) * 256, :] = before(i)
+    seen = dot_nt(patches_v[last, :, 0:256], proj_v[0].reshape(width, 256))
+    for k in range(1, 4):
+        seen = seen + dot_nt(patches_v[last, :, k * 256 : (k + 1) * 256], proj_v[k].reshape(width, 256))
+    q_v[...] = seen.astype(BF16)
+    front(last, True)
 
     n_early = len(sent)
 
@@ -306,8 +321,7 @@
     order = [(x + i) % NX for i in DXS] + [x]
     pair_cp = []
     for i, xb in enumerate(order):
-        at = pl.ds(pl.multiple_of(xb * 256, 256), 256)
-        g = grad_v[at, :] + dot_tn(recv_v[last, :, :, at].reshape(n_slots, 256), dq_v[last])
+        g = (grad_v[i * 256 : (i + 1) * 256, :] if i < 3 else before(i)) + dot(turned_v[ats[i], :], dq_v[last])
         pair_s[i] = g[:, half:].astype(BF16)
         pair_cp.append(go(remote(pair_s.at[i], pair_r.at[i], pair_ss.at[i], pair_rs.at[i], to_seq(0, 1))))
         sum_v[i] = g[:, :half]
@@ -369,31 +383,44 @@
         cp.wait_recv()
     a_f[...] = part(3, 0) + a_r[0].astype(F32) + a_r[1].astype(F32)
     a2_cp, b2_cp = [], []
+    zs = [(z + r) % NZ for r in ZFAR]
+
+    def by_half(src, dst, ss, rs, dev):
+        return [
+            go(remote(src.at[4 * u : 4 * u + 4], dst.at[4 * u : 4 * u + 4], ss.at[u], rs.at[u], dev)) for u in range(2)
+        ]
+
     for j in range(3):
-        a2_s[j] = a_f[:, :, ycols(DYS[j])].astype(BF16)
-        a2_cp.append(go(remote(a2_s.at[j], a2_r.at[j], a2_ss.at[j], a2_rs.at[j], to_seq(DYS[j], 0))))
+        for n, zb in enumerate(zs):
+            a2_s[j, n] = a_f[zb, :, ycols(DYS[j])].astype(BF16)
+        a2_cp.append(by_half(a2_s.at[j], a2_r.at[j], a2_ss.at[j], a2_rs.at[j], to_seq(DYS[j], 0)))
     for cp in bd_cp + bm_cp:
         cp.wait_recv()
     for i in range(NX):
         left = jnp.concatenate([b_r[0, 1, i], b_r[0, 0, i]], axis=0).astype(F32)
         right = jnp.concatenate([b_r[1, 0, i], b_r[1, 1, i]], axis=0).astype(F32)
-        acc_b = part(i, 1, ycols(0)) + left + right
+        b_f[i] = part(i, 1, ycols(0)) + left + right
         if i < 3:
-            b2_s[i] = acc_b.astype(BF16)
-            b2_cp.append(go(remote(b2_s.at[i], b2_r.at[i], b2_ss.at[i], b2_rs.at[i], to_x(DXS[i]))))
-    acc_a = a_f[:, :, ycols(0)]
+            for n, zb in enumerate(zs):
+                b2_s[i, n] = b_f[i, zb].astype(BF16)
+            b2_cp.append(by_half(b2_s.at[i], b2_r.at[i], b2_ss.at[i], b2_rs.at[i], to_x(DXS[i])))
     n_mid = len(sent)
-    for cp in a2_cp + b2_cp:
-        cp.wait_recv()
-    for j in range(3):
-        acc_a = acc_a + a2_r[j].astype(F32)
-        acc_b = acc_b + b2_r[j].astype(F32)
-    z3_f[:, 0:16, :] = acc_a
-    z3_f[:, 16:32, :] = acc_b
-    z3_s[...] = z3_f[...].astype(BF16)
     z3_cp = []
-    for i in range(1, NZ):
-        z3_cp.append(go(remote(z3_s.at[(z + i) % NZ], z3_r.at[i - 1], z3_ss.at[i - 1], z3_rs.at[i - 1], to_z(i))))
+    for u in range(2):
+        for cp in a2_cp + b2_cp:
+            cp[u].wait_recv()
+        for n in range(4 * u, 4 * u + 4):
+            acc_a, acc_b = a_f[zs[n], :, ycols(0)], b_f[3, zs[n]]
+            for j in range(3):
+                acc_a = acc_a + a2_r[j, n].astype(F32)
+                acc_b = acc_b + b2_r[j, n].astype(F32)
+            if ZFAR[n] == 0:
+                z3_f[0:16, :] = acc_a
+                z3_f[16:32, :] = acc_b
+            else:
+                z3_s[n, 0:16, :] = acc_a.astype(BF16)
+                z3_s[n, 16:32, :] = acc_b.astype(BF16)
+                z3_cp.append(go(remote(z3_s.at[n], z3_r.at[n], z3_ss.at[n], z3_rs.at[n], to_z(ZFAR[n]))))
     for cp in loss_cp:
         cp.wait_recv()
     loss_o[...] = loss_s[s] + jnp.sum(loss_r[...], axis=0)
@@ -401,7 +428,7 @@
         cp.wait_send()
     for cp in z3_cp:
         cp.wait_recv()
-    grad_o[...] = z3_f[z] + jnp.sum(z3_r[...].astype(F32), axis=0)
+    grad_o[...] = z3_f[...] + jnp.sum(z3_r[...].astype(F32), axis=0)
     for cp in sent[n_mid:]:
         cp.wait_send()
 
@@ -420,7 +447,7 @@
     dma = pltpu.SemaphoreType.DMA
     any_ = pl.BlockSpec(memory_space=pl.ANY)
     vmem = pl.BlockSpec(memory_space=pltpu.VMEM)
-    pairs = [(pages, 7), (7,), (NZ + 3,), (NZ + 2,), (NX + NZ,), (7,), (4,), (2, 2), (2,), (2, 2, 4), (2, 4), (3,), (3,), (7,)]
+    pairs = [(pages, 7), (7,), (NZ + 3,), (NZ + 2,), (NX + NZ,), (7,), (4,), (2, 2), (2,), (2, 2, 4), (2, 4), (3, 2), (3, 2), (7,)]
     loss, grad = pl.pallas_call(
         kernel,
         out_shape=(vm((pages, wdev), F32), vm((width // (NX * NZ), width // NSEQ), F32)),
@@ -439,6 +466,7 @@
             vm((NSEQ, 2 * pages, wdev), I32),
             vm((NSEQ, pages, wdev), I32),
             vm((NSEQ, pages, wdev), F32),
+            vm((width, NSEQ * cap), BF16),
             vm((width, width), F32),
             vm((pages, NSEQ * cap, ppsz), BF16),
             vm((pages, NSEQ * cap, 1), I32),
@@ -462,7 +490,8 @@
             vm((3, NZ, 16, 128), BF16),
             vm((3, NZ, 16, 128), BF16),
             vm((3, NZ, 16, 128), BF16),
-            vm((NZ, 32, 128), F32),
+            vm((NX, NZ, 16, 128), F32),
+            vm((32, 128), F32),
             vm((NZ, 32, 128), BF16),
             vm((7, 32, 128), BF16),
             dma((pages + 7,)),

time: 57.3 us -> 56.6 us (0.988)
  Pallas kernels: 56.6 us -> 55.6 us
    pallas_call x1, Pallas kernels: 56 us -> 55 us  [local(): pl.pallas_call(kernel, out_shape=(vm((pages, wdev), F32), vm((width // (N...]
where the time goes in v3:
time: 56.6 us; the launch traced here: 56.3 us
  Pallas kernels  55.6 us (98%)
  between operations  0.64 us (1%)
    pallas_call x1, Pallas kernels, local(): pl.pallas_call(kernel, out_shape=(vm((pages, wdev), F32), vm((width // (N...  55 us

profile of v3, /device:TPU:24, one launch (start us, length us, event | category | flops | bytes accessed | tf_op | source)
XLA Modules:
  0.0 56.3 jit_solution(12744165339363579066)
XLA Ops:
  0.6 55.0 %grounding.1 = (f32[4,128]{1,0:T(4,128)S(1)}, f32[32,128]{1,0:T(8,128)S(1)}) custom-call(bf16[4,128,1024]{2,1,0:T(8,128)(2,1)} %words_h.1, bf16[4,256,1024]{2,1,0:T(8,128)(2,1)} %patches_h.1, bf16[32,1024]{1,0:T(8,128)(2,1)} %proj_h.1, s32[4,128]{1,0:T(4,128)} %bitcast.1, s32[4,128]{1,0:T(4,128)} %targets_h.1, s32[4]{0:T(128)} %counts_h.1, s32[4,16,32]{2,1,0:T(8,128)} %flags_h.1), custom_call_target="tpu_custom_call" | custom-call | tf_op jit(solution)/shard_map/grounding/pallas_call | solution.py:451
  55.6 0.6 %finish.1 = (f32[4,128]{1,0:T(4,128)}, f32[32,128]{1,0:T(8,128)}) custom-call(f32[4,128]{1,0:T(4,128)S(1)} %get-tuple-element.4.loss_r, f32[32,128]{1,0:T(8,128)S(1)} %get-tuple-element.5.grad_r), custom_call_target="tpu_custom_call" | custom-call | tf_op jit(solution)/shard_map/finish/pallas_call | solution.py:503

commit v4 on v3

--- a/solution.py
+++ b/solution.py
@@ -79,7 +79,7 @@
         return cp
 
     barrier = pltpu.get_barrier_semaphore()
-    greet = [to_seq(*t) for t in PEERS] + [to_x(i) for i in DXS] + [to_z(i) for i in range(1, NZ)]
+    greet = [to_z(i) for i in ZORDER[:3]] + [to_seq(*t) for t in PEERS] + [to_z(i) for i in ZORDER[3:]] + [to_x(i) for i in DXS]
     for dev in greet:
         pl.semaphore_signal(barrier, inc=1, device_id=dev, device_id_type=MESH)
 
@@ -167,9 +167,6 @@
         ref = proj_v.at[2 * c + 1, :, zrows((z + i) % NZ)]
         return remote(ref, ref, sib_ss.at[NX + i], sib_rs.at[NX + i], to_seq(0, 1))
 
-    meta_cp = []
-    for i, (dy, dc) in enumerate(PEERS):
-        meta_cp.append(go(remote(meta_v.at[s], meta_v.at[s], meta_ss.at[i], meta_rs.at[i], to_seq(dy, dc))))
     send_page(0)
     for i in range(2):
         loads[pages + i].wait()
@@ -177,6 +174,9 @@
         go(ag_b(0, i))
     for i in range(1, NZ):
         go(ag_a(0, i))
+    meta_cp = []
+    for i, (dy, dc) in enumerate(PEERS):
+        meta_cp.append(go(remote(meta_v.at[s], meta_v.at[s], meta_ss.at[i], meta_rs.at[i], to_seq(dy, dc))))
     build(1)
     send_page(1)
     build(2)

time: 56.6 us -> 56.6 us (level)
  no operation moved by 1% of the time
where the time goes in v4:
time: 56.6 us
  Pallas kernels  55.9 us (99%)
  between operations  0.64 us (1%)
    pallas_call x1, Pallas kernels, local(): pl.pallas_call(kernel, out_shape=(vm((pages, wdev), F32), vm((width // (N...  55.3 us

profile of v4, /device:TPU:24, one launch (start us, length us, event | category | flops | bytes accessed | tf_op | source)
XLA Modules:
  0.0 56.6 jit_solution(2457013749008454027)
XLA Ops:
  0.6 55.3 %grounding.1 = (f32[4,128]{1,0:T(4,128)S(1)}, f32[32,128]{1,0:T(8,128)S(1)}) custom-call(bf16[4,128,1024]{2,1,0:T(8,128)(2,1)} %words_h.1, bf16[4,256,1024]{2,1,0:T(8,128)(2,1)} %patches_h.1, bf16[32,1024]{1,0:T(8,128)(2,1)} %proj_h.1, s32[4,128]{1,0:T(4,128)} %bitcast.1, s32[4,128]{1,0:T(4,128)} %targets_h.1, s32[4]{0:T(128)} %counts_h.1, s32[4,16,32]{2,1,0:T(8,128)} %flags_h.1), custom_call_target="tpu_custom_call" | custom-call | tf_op jit(solution)/shard_map/grounding/pallas_call | solution.py:451
  55.9 0.6 %finish.1 = (f32[4,128]{1,0:T(4,128)}, f32[32,128]{1,0:T(8,128)}) custom-call(f32[4,128]{1,0:T(4,128)S(1)} %get-tuple-element.4.loss_r, f32[32,128]{1,0:T(8,128)S(1)} %get-tuple-element.5.grad_r), custom_call_target="tpu_custom_call" | custom-call | tf_op jit(solution)/shard_map/finish/pallas_call | solution.py:503
